TPU v7x, 128 devices: a whole 4x4x4 slice. The times are simulated.
128 devices in a mesh: blk: 16 (over x_hi, z, core), tile: 8 (over x_lo, y).
Axes of the slice: x: 4 (x_hi: 2, x_lo: 2; x = x_hi * 2 + x_lo), y: 4, z: 4, core: 2. Of those that a mesh axis runs over, the one named last changes fastest.
Arguments:
- features: bfloat16 [8192, 8192], P('tile', 'blk'), may hold values from -6 to 6
- weight_kv: bfloat16 [8192, 12288], P(None, 'blk'), may hold values from -0.0625 to 0.0625
- key_gain: float32 [6, 128], replicated, may hold values from 0.1 to 1.9
- block_reader: int32 [64], P('tile'), may hold values from 0 to 7, as said below
Outputs:
- routed_kv: bfloat16 [32768, 12288], P('tile', 'blk')
Inputs may be any that keep to these rules, and one draw needn't show every extreme that they name: `block_reader`: at most 4 of the 8 blocks of one index of tile name the same reader, and one reader is named by exactly 4 blocks of every index of tile.
All inputs are finite; a program needn't handle non-finite values.
Results may differ from a plain program's by a relative error of at most 0.001.
Values may be sent and summed in bfloat16 or wider, within the bound.
A program may use at most 192 MiB of HBM per device.

v0:
```python
import jax
import jax.numpy as jnp
from jax import lax
from jax.sharding import PartitionSpec as P

KVH = 8
HD = 128
L = 6
BT = 128
CAP = 4
norm_eps = 1e-05


def local_slots(readers, tile_count):
    onehot = (readers[:, None] == jnp.arange(tile_count, dtype=jnp.int32)[None, :]).astype(
        jnp.int32
    )
    earlier = jnp.cumsum(onehot, axis=0) - onehot
    slot_rank = jnp.sum(earlier * onehot, axis=1)
    return readers * CAP + slot_rank


def shards(features, weight_kv, key_gain, block_reader):
    row_count, feat_local = features.shape
    col_count = weight_kv.shape[1]
    pair_count = col_count // (2 * HD)
    tile_count = lax.axis_size("tile")
    block_count = row_count // BT
    layer_ids = (
        lax.axis_index("blk") * pair_count + jnp.arange(pair_count, dtype=jnp.int32)
    ) // KVH
    layer_pick = (layer_ids[:, None] == jnp.arange(L, dtype=jnp.int32)[None, :]).astype(jnp.float32)
    key_gains = jnp.dot(layer_pick, key_gain, precision=lax.Precision.HIGHEST)
    slot_index = local_slots(block_reader, tile_count)
    selector = (
        slot_index[None, :] == jnp.arange(tile_count * CAP, dtype=jnp.int32)[:, None]
    ).astype(jnp.bfloat16)
    slot_rows = tile_count * CAP * BT
    running = jnp.dot(
        lax.all_gather(features, "blk", axis=1, tiled=True),
        weight_kv,
        preferred_element_type=jnp.float32,
    )
    count = running.shape[0]
    halves = running.reshape(count, pair_count, 2, HD)
    key_part = halves[:, :, 0]
    mean_square = jnp.mean(key_part * key_part, axis=-1, keepdims=True)
    key_part = key_part * lax.rsqrt(mean_square + norm_eps) * key_gains[None]
    joined = jnp.stack([key_part, halves[:, :, 1]], axis=2)
    key_value = joined.reshape(count, col_count).astype(jnp.bfloat16)
    outgoing = jnp.dot(
        selector, key_value.reshape(block_count, BT * col_count), preferred_element_type=jnp.float32
    )
    outgoing = outgoing.astype(jnp.bfloat16).reshape(slot_rows, col_count)
    routed = lax.all_to_all(outgoing, "tile", split_axis=0, concat_axis=0, tiled=True)
    return routed


def solution(mesh):
    return jax.shard_map(
        shards,
        mesh=mesh,
        in_specs=(P("tile", "blk"), P(None, "blk"), P(), P("tile")),
        out_specs=P("tile", "blk"),
        check_vma=False,
    )
```

profile of v0, /device:TPU:0, one launch (start us, length us, event | category | flops | bytes accessed | tf_op | source)
XLA Modules:
  0.0 278.6 jit_solution(7639619202823156865)
XLA Ops:
  6.5 0.0 copy-start
  6.5 0.0 all-gather.2.cloned.1.call-start
  6.5 0.7 all-gather.2.cloned.1.call-update
  7.3 0.7 fusion.1
  8.0 0.8 select_reduce_fusion
  8.9 0.7 multiply_add_fusion
  9.5 0.0 copy-done
  9.5 0.2 fusion.2
  9.7 121.5 %all-gather.2.cloned.1.call-done = bf16[1024,8192]{1,0:T(8,128)(2,1)} async-done(((bf16[1024,512]{1,0:T(8,128)(2,1)}), bf16[1024,8192]{1,0:T(8,128)(2,1)}) %all-gather.2.cloned.1.call-update) | async-done | bytes 16777232 | tf_op jit(solution)/shard_map/all_gather | solution.py:40
  131.2 20.3 %fusion.4 = f32[1024,768]{0,1:T(8,128)} fusion(bf16[1024,8192]{1,0:T(8,128)(2,1)} %all-gather.2.cloned.1.call-done, bf16[8192,768]{1,0:T(8,128)(2,1)} %param.5), kind=kOutput, calls=%fused_computation.18 | convolution fusion | flops 12884901888 | bytes 32505856 | tf_op jit(solution)/shard_map/dot_general | solution.py:39
  151.5 1.5 slice.9
  153.0 2.4 slice.10
  155.4 1.7 copy.16
  157.2 5.7 %multiply_reduce_fusion = f32[1024,3]{1,0:T(8,128)S(1)} fusion(f32[1024,3,1,128]{3,2,1,0:T(1,128)S(1)} %copy.16), kind=kLoop, calls=%fused_computation.3 | loop fusion | flops 783360 | bytes 1585152 | tf_op jit(solution)/shard_map/reduce_sum | solution.py:47
  162.9 0.9 add_rsqrt_fusion
  163.8 4.1 %copy.17 = bf16[1024,3,1,128]{3,2,1,0:T(2,128)(2,1)S(1)} copy(bf16[1024,3,1,128]{0,3,2,1:T(8,128)(2,1)} %slice.10) | data formatting | bytes 1572864
  167.9 8.0 %multiply_convert_fusion = bf16[1024,3,1,128]{3,2,1,0:T(2,128)(2,1)S(1)} fusion(f32[1024,3,1,128]{3,2,1,0:T(1,128)S(1)} %copy.16, f32[3,128]{1,0:T(4,128)S(1)} %fusion.2, f32[1024,3]{1,0:T(8,128)} %add_rsqrt_fusion), kind=kLoop, calls=%fused_computation.2 | loop fusion | flops 1179648 | bytes 2373120 | tf_op jit(solution)/shard_map/convert
  176.0 3.6 %pad_maximum_fusion = bf16[1024,3,2,128]{3,2,1,0:T(2,128)(2,1)S(1)} fusion(bf16[1024,3,1,128]{3,2,1,0:T(2,128)(2,1)S(1)} %copy.17, bf16[1024,3,1,128]{3,2,1,0:T(2,128)(2,1)S(1)} %multiply_convert_fusion), kind=kLoop, calls=%fused_computation.1 | loop fusion | flops 3145728 | bytes 3145728 | tf_op jit(solution)/shard_map/stack | solution.py:49
  179.6 1.2 convert_element_type.14
  180.8 4.5 %convolution_convert_fusion = bf16[32,98304]{1,0:T(8,128)(2,1)} fusion(bf16[8,98304]{1,0:T(8,128)(2,1)S(1)} %convert_element_type.14, s32[8]{0:T(128)S(1)} %multiply_add_fusion), kind=kOutput, calls=%fused_computation | convolution fusion | flops 53477632 | bytes 7864352 | tf_op jit(solution)/shard_map/dot_general | solution.py:51
  185.3 7.3 %all_to_all.8 = bf16[8,512,768]{2,1,0:T(8,128)(2,1)} reshape(bf16[32,98304]{1,0:T(8,128)(2,1)} %convolution_convert_fusion) | data formatting | bytes 12582912 | tf_op jit(solution)/shard_map/all_to_all | solution.py:55
  192.5 76.5 %all_to_all.12 = bf16[8,512,768]{2,1,0:T(8,128)(2,1)S(1)} all-to-all(bf16[8,512,768]{2,1,0:T(8,128)(2,1)} %all_to_all.8), channel_id=1, replica_groups=mesh['blk'=16,'tile'=8] {'tile'}, dimensions={0} | all-to-all | bytes 12582912 | tf_op jit(solution)/shard_map/all_to_all | solution.py:55
  269.1 0.0 copy-start.1
  269.1 2.7 copy.20
  271.8 0.0 copy-done.1
  (2 shorter events, 0.0 us)
Async XLA Ops:
  6.5 3.0 %copy-start = (f32[6,128]{1,0:T(8,128)S(1)}, f32[6,128]{1,0:T(8,128)}, u32[]{:S(2)}) copy-start(f32[6,128]{1,0:T(8,128)} %param.6) | copy-start | bytes 9220
  6.5 124.7 %all-gather.2.cloned.1.call-start = ((), (), s32[]{:S(2)}) async-start(), calls=%async_computation.1 | async-start | bytes 17825792 | tf_op jit(solution)/shard_map/all_gather | solution.py:40
  269.1 2.7 copy-start.1
Sparse Core Ops, SparseCore 0:
  9.6 121.5 all-gather.1
where the time goes:
time: 279 us
  waiting for transfers between devices  122 us (44%)
  blocking collectives  76.5 us (27%)
  matrix products  24.9 us (9%)
  local copies, waits for them, and re-layouts  21 us (8%)
  other arithmetic  20.5 us (7%)
  between operations  13.4 us (5%)
    all_gather x1, waiting for transfers between devices, shards(): lax.all_gather(features, 'blk', axis=1, tiled=True)  122 us
    all_to_all x1, blocking collectives, shards(): lax.all_to_all(outgoing, 'tile', split_axis=0, concat_axis=0, tiled=True)  76.5 us
    dot_general x1, matrix products, shards(): jnp.dot(lax.all_gather(features, 'blk', axis=1, tiled=True), weight_kv, p...  20.3 us
    unnamed x7, local copies, waits for them, and re-layouts  8.58 us
    another operation x1, other arithmetic  8.05 us
    all_to_all x1, local copies, waits for them, and re-layouts, shards(): lax.all_to_all(outgoing, 'tile', split_axis=0, concat_axis=0, tiled=True)  7.28 us
    reduce_sum x1, other arithmetic, shards(): mean_square = jnp.mean(key_part * key_part, axis=-1, keepdims=True)  5.71 us
  transfers between devices with their start and end apart: 1, of which 1 were waited for; matrix products, arithmetic and copies ran while one was open for 1% of the time, Pallas kernels for 0%

commit v1 on v0

--- a/solution.py
+++ b/solution.py
@@ -9,6 +9,12 @@
 BT = 128
 CAP = 4
 norm_eps = 1e-05
+
+
+def matrix_convert(v0):
+    val = lax.axis_size("blk")
+    y1 = jnp.concatenate(lax.all_to_all(jnp.stack(val * [v0], 0), "blk", 0, 0), axis=1)
+    return y1
 
 
 def local_slots(readers, tile_count):
@@ -36,11 +42,7 @@
         slot_index[None, :] == jnp.arange(tile_count * CAP, dtype=jnp.int32)[:, None]
     ).astype(jnp.bfloat16)
     slot_rows = tile_count * CAP * BT
-    running = jnp.dot(
-        lax.all_gather(features, "blk", axis=1, tiled=True),
-        weight_kv,
-        preferred_element_type=jnp.float32,
-    )
+    running = jnp.dot(matrix_convert(features), weight_kv, preferred_element_type=jnp.float32)
     count = running.shape[0]
     halves = running.reshape(count, pair_count, 2, HD)
     key_part = halves[:, :, 0]

time: 279 us -> 436 us (1.56); the launches traced: 279 us -> 428 us
  waiting for transfers between devices: 122 us -> 239 us
  local copies, waits for them, and re-layouts: 21 us -> 80.1 us
  other arithmetic: 20.5 us -> 0.82 us
  between operations: 13.4 us -> 0.08 us
  starting transfers between devices: 0.01 us -> 8.01 us
    all_to_all x0 -> x1, waiting for transfers between devices: none -> 239 us  [matrix_convert(): lax.all_to_all(jnp.stack(val * [v0], 0), 'blk', 0, 0)]
    all_gather x1 -> x0, waiting for transfers between devices: 122 us -> none  [shards(): lax.all_gather(features, 'blk', axis=1, tiled=True)]
    reshape x0 -> x2, local copies, waits for them, and re-layouts: none -> 44.1 us  [matrix_convert(): jnp.concatenate(lax.all_to_all(jnp.stack(val * [v0], 0), 'blk', 0, 0), ax...]
    dot_general x0 -> x1, local copies, waits for them, and re-layouts: none -> 15.7 us  [shards(): jnp.dot(matrix_convert(features), weight_kv, preferred_element_type=jnp.f...]
    another operation x0 -> x2, local copies, waits for them, and re-layouts: none -> 9.04 us  [the longest x1 6.81 us: matrix_convert(): jnp.stack(val * [v0], 0)]
    all_to_all x0 -> x1, starting transfers between devices: none -> 8.01 us  [matrix_convert(): lax.all_to_all(jnp.stack(val * [v0], 0), 'blk', 0, 0)]
    another operation x1, other arithmetic: 8.05 us -> 0.2 us
    unnamed x7, local copies, waits for them, and re-layouts: 8.58 us -> 2.72 us
  transfers between devices with their start and end apart: 1 -> 1, of which waited for: 1 -> 1; matrix products, arithmetic and copies ran while one was open for 1% -> 4% of each run, Pallas kernels for 0% -> 0%
where the time goes in v1:
time: 436 us; the launch traced here: 428 us
  waiting for transfers between devices  239 us (55%)
  local copies, waits for them, and re-layouts  80.1 us (18%)
  blocking collectives  77.1 us (18%)
  matrix products  23.2 us (5%)
  starting transfers between devices  8.01 us (2%)
    all_to_all x1, waiting for transfers between devices, matrix_convert(): lax.all_to_all(jnp.stack(val * [v0], 0), 'blk', 0, 0)  239 us
    all_to_all x1, blocking collectives, shards(): lax.all_to_all(outgoing, 'tile', split_axis=0, concat_axis=0, tiled=True)  77.1 us
    reshape x2, local copies, waits for them, and re-layouts, matrix_convert(): jnp.concatenate(lax.all_to_all(jnp.stack(val * [v0], 0), 'blk', 0, 0), ax...  44.1 us
    dot_general x1, matrix products, shards(): jnp.dot(matrix_convert(features), weight_kv, preferred_element_type=jnp.f...  18.6 us
    dot_general x1, local copies, waits for them, and re-layouts, shards(): jnp.dot(matrix_convert(features), weight_kv, preferred_element_type=jnp.f...  15.7 us
  transfers between devices with their start and end apart: 1, of which 1 were waited for; matrix products, arithmetic and copies ran while one was open for 4% of the time, Pallas kernels for 0%

profile of v1, /device:TPU:0, one launch (start us, length us, event | category | flops | bytes accessed | tf_op | source)
XLA Modules:
  0.0 428.2 jit_solution(8310165232132085558)
XLA Ops:
  0.0 0.0 copy-start
  0.0 6.8 %stack.5 = bf16[16,1024,512]{2,1,0:T(8,128)(2,1)} broadcast(bf16[1024,512]{1,0:T(8,128)(2,1)} %param.4), dimensions={1,2} | broadcast | bytes 17825792 | tf_op jit(solution)/shard_map/stack | solution.py:16
  6.8 8.0 %all-to-all-start = ((bf16[16,1024,512]{2,1,0:T(8,128)(2,1)}), bf16[16,1024,512]{2,1,0:T(8,128)(2,1)}, u32[]{:S(2)}, u32[]{:S(2)}) async-start(bf16[16,1024,512]{2,1,0:T(8,128)(2,1)} %stack.5), calls=%async_computation | async-start | bytes 33554432 | tf_op jit(solution)/shard_map/all_to_all | solution.py:16
  14.8 0.0 copy-start.2
  14.8 15.7 %copy.15 = bf16[768,8192]{1,0:T(8,128)(2,1)} copy(bf16[768,8192]{0,1:T(8,128)(2,1)} %bitcast.11) | data formatting | bytes 25165824 | tf_op jit(solution)/shard_map/dot_general | solution.py:45
  30.6 0.0 copy-done.2
  30.6 0.1 fusion.3
  30.7 0.2 select_reduce_fusion
  30.9 0.0 copy-done
  30.9 0.2 fusion.4
  31.1 238.9 %all-to-all-done = bf16[16,1024,512]{2,1,0:T(8,128)(2,1)} async-done(((bf16[16,1024,512]{2,1,0:T(8,128)(2,1)}), bf16[16,1024,512]{2,1,0:T(8,128)(2,1)}, u32[]{:S(2)}, u32[]{:S(2)}) %all-to-all-start) | async-done | bytes 16777248 | tf_op jit(solution)/shard_map/all_to_all | solution.py:16
  269.9 18.5 %copy.11 = bf16[1024,16,512]{2,1,0:T(8,128)(2,1)} copy(bf16[1024,16,512]{2,0,1:T(8,128)(2,1)} %bitcast) | data formatting | bytes 33554432 | tf_op jit(solution)/shard_map/reshape | solution.py:16
  288.4 25.6 %reshape.51 = bf16[1024,8192,1,1]{1,0,2,3:T(8,128)(2,1)} reshape(bf16[1024,16,512]{2,1,0:T(8,128)(2,1)} %copy.11) | data formatting | bytes 33554432 | tf_op jit(solution)/shard_map/reshape | solution.py:16
  314.0 18.6 %fusion = f32[1024,3,2,128]{0,3,2,1:T(8,128)S(1)} fusion(bf16[3,2,128,8192]{3,2,1,0:T(8,128)(2,1)} %bitcast.12, bf16[1024,8192,1,1]{1,0,2,3:T(8,128)(2,1)} %reshape.51), kind=kOutput, calls=%fused_computation.1 | convolution fusion | flops 12884901888 | bytes 32505856 | tf_op jit(solution)/shard_map/dot_general | solution.py:45
  332.6 0.2 multiply_reduce_fusion
  332.7 0.1 slice.14
  332.9 0.2 multiply_convert_fusion
  333.1 0.1 pad_maximum_fusion
  333.2 2.2 copy.13
  335.5 1.2 convert_element_type.14
  336.7 4.5 %convolution_convert_fusion = bf16[32,98304]{1,0:T(8,128)(2,1)} fusion(bf16[8,98304]{1,0:T(8,128)(2,1)S(1)} %convert_element_type.14, s32[8]{0:T(128)S(1)} %multiply_add_fusion), kind=kOutput, calls=%fused_computation | convolution fusion | flops 53477632 | bytes 7864352 | tf_op jit(solution)/shard_map/dot_general | solution.py:53
  341.1 7.3 %all_to_all.12 = bf16[8,512,768]{2,1,0:T(8,128)(2,1)} reshape(bf16[32,98304]{1,0:T(8,128)(2,1)} %convolution_convert_fusion) | data formatting | bytes 12582912 | tf_op jit(solution)/shard_map/all_to_all | solution.py:57
  348.4 77.1 %all_to_all.17 = bf16[8,512,768]{2,1,0:T(8,128)(2,1)S(1)} all-to-all(bf16[8,512,768]{2,1,0:T(8,128)(2,1)} %all_to_all.12), channel_id=1, replica_groups=mesh['blk'=16,'tile'=8] {'tile'}, dimensions={0} | all-to-all | bytes 12582912 | tf_op jit(solution)/shard_map/all_to_all | solution.py:57
  425.5 0.0 copy-start.1
  425.5 2.7 copy.17
  428.2 0.0 copy-done.1
  (4 shorter events, 0.1 us)
Async XLA Ops:
  0.0 30.9 %copy-start = (f32[6,128]{1,0:T(8,128)S(1)}, f32[6,128]{1,0:T(8,128)}, u32[]{:S(2)}) copy-start(f32[6,128]{1,0:T(8,128)} %param.6) | copy-start | bytes 9220
  6.8 263.1 %all-to-all-start = ((bf16[16,1024,512]{2,1,0:T(8,128)(2,1)}), bf16[16,1024,512]{2,1,0:T(8,128)(2,1)}, u32[]{:S(2)}, u32[]{:S(2)}) async-start(bf16[16,1024,512]{2,1,0:T(8,128)(2,1)} %stack.5), calls=%async_computation | async-start | bytes 33554432 | tf_op jit(solution)/shard_map/all_to_all | solution.py:16
  14.8 15.7 %copy-start.2 = (s32[8]{0:T(128)S(1)}, s32[8]{0:T(128)}, u32[]{:S(2)}) copy-start(s32[8]{0:T(128)} %param.7) | copy-start | bytes 100
  425.5 2.7 copy-start.1
